TPU v7x, 128 devices: a whole 4x4x4 slice. The times are simulated.
128 devices in a mesh: grp: 2 (over core), pts: 64 (over z, x, y).
Axes of the slice: x: 4, y: 4, z: 4, core: 2. Of those that a mesh axis runs over, the one named last changes fastest.
Arguments:
- element_attribute_table: bfloat16 [1048576, 512], P(('grp', 'pts')), parts along dimension 0, may hold values from -16 to 16
- active_group_tally: int32 [128], P(('grp', 'pts')), parts along dimension 0, may hold values from 48 to 64, as said below
- group_destination_part: int32 [8192], P(('grp', 'pts')), parts along dimension 0, may hold values from 0 to 63, as said below
- element_vertex_permutation: int32 [8192, 128], P(('grp', 'pts')), parts along dimension 0, may hold values from 0 to 127, each once within a row
- softness_factor: float32 [8], replicated, may hold values from 0.15 to 0.6
- entry_projection_coefficients: bfloat16 [512, 1024], replicated, may hold values from -0.25 to 0.25
- partition_score_coefficients: bfloat16 [8, 64, 256], replicated, may hold values from -0.75 to 0.75
- summary_query_key_coefficients: bfloat16 [64, 192], replicated, may hold values from -0.75 to 0.75
- final_projection_coefficients: bfloat16 [512, 512], replicated, may hold values from -0.25 to 0.25
Outputs:
- point_features: bfloat16 [1048576, 512], P(('grp', 'pts')), parts along dimension 0
There are 2 independent parts, one for each index of `grp`. A program takes and returns all parts, laid end to end along the dimension named above; an argument that names none is the same for every part. Nothing has to cross between parts.
Inputs may be any that keep to these rules, and one draw needn't show every extreme that they name: The live blocks of a device are its first active_group_tally slots; some device has all 64 live. `group_destination_part`: no device names a point shard in more than 1 of its slots; some point shard is named exactly 1 times by the live blocks of every device. `element_vertex_permutation`: each row is a permutation.
All inputs are finite; a program needn't handle non-finite values.
Results may differ from a plain program's by a relative error of at most 0.0016.
Values may be sent and summed in bfloat16 or wider, within the bound.
A program may use at most 192 MiB of HBM per device.

v0:
```python
import math

import jax
import jax.numpy as jnp
from jax import lax
from jax.sharding import PartitionSpec as P

NORM_EPS = 1e-05
SLICE_EPS = 1e-05


def normalize_rows(point_rows):
    values = point_rows.astype(jnp.float32)
    centre = jnp.mean(values, axis=-1, keepdims=True)
    spread = jnp.mean(jnp.square(values - centre), axis=-1, keepdims=True)
    return ((values - centre) * lax.rsqrt(spread + NORM_EPS)).astype(jnp.bfloat16)


def project_rows(point_rows, entry_projection_coefficients):
    channels = point_rows.shape[-1]
    mixed = jnp.dot(
        normalize_rows(point_rows),
        entry_projection_coefficients,
        preferred_element_type=jnp.float32,
    )
    return (mixed[:, :channels].astype(jnp.bfloat16), mixed[:, channels:].astype(jnp.bfloat16))


def slice_attention(tokens, summary_query_key_coefficients):
    head_width = tokens.shape[-1]
    project = jnp.einsum(
        "hsd,de->hse",
        tokens,
        summary_query_key_coefficients.astype(jnp.float32),
        precision=lax.Precision.HIGHEST,
    )
    queries = project[..., :head_width]
    slice_keys = project[..., head_width : 2 * head_width]
    slice_values = project[..., 2 * head_width :]
    scores = jnp.einsum(
        "hsd,htd->hst", queries, slice_keys, precision=lax.Precision.HIGHEST
    ) * head_width ** (-0.5)
    powered_entries = jnp.exp(scores)
    attend = powered_entries / jnp.sum(powered_entries, axis=-1, keepdims=True)
    return jnp.einsum("hst,htd->hsd", attend, slice_values, precision=lax.Precision.HIGHEST).astype(
        jnp.bfloat16
    )


def finish_layer(
    point_rows,
    feature_matrix,
    middle_result,
    live_mask,
    block_feature_rows,
    softness_factor,
    partition_score_coefficients,
    summary_query_key_coefficients,
    final_projection_coefficients,
):
    total_rows, channels = point_rows.shape
    head_count, head_width, slice_count = partition_score_coefficients.shape
    units = total_rows // block_feature_rows
    group = math.gcd(units, 8)
    step_rows = group * block_feature_rows
    step_count = units // group
    middle_steps = middle_result.reshape(step_count, step_rows, head_count, head_width)

    def weigh(middle_part):
        partition_raw_scores = jnp.einsum(
            "rhd,hds->rhs",
            middle_part,
            partition_score_coefficients,
            preferred_element_type=jnp.float32,
        )
        powered_entries = jnp.exp(partition_raw_scores / softness_factor[None, :, None])
        return (powered_entries / jnp.sum(powered_entries, axis=-1, keepdims=True)).astype(
            jnp.bfloat16
        )

    weights = lax.map(weigh, middle_steps)
    masked = weights * live_mask.reshape(step_count, step_rows, 1, 1).astype(jnp.bfloat16)
    feature_steps = feature_matrix.reshape(step_count, step_rows, head_count, head_width)
    numer = jnp.einsum("nrhs,nrhd->hsd", masked, feature_steps, preferred_element_type=jnp.float32)
    denom = jnp.sum(masked, axis=(0, 1), dtype=jnp.float32)
    numer, denom = lax.psum((numer, denom), "pts")
    tokens = numer / (denom[..., None] + SLICE_EPS)
    mixed_tokens = slice_attention(tokens, summary_query_key_coefficients)
    spread_back = jnp.einsum(
        "nrhs,hsd->nrhd", weights, mixed_tokens, preferred_element_type=jnp.float32
    )
    spread_back = spread_back.astype(jnp.bfloat16).reshape(total_rows, channels)
    update = jnp.dot(spread_back, final_projection_coefficients, preferred_element_type=jnp.float32)
    return ((point_rows.astype(jnp.float32) + update) * live_mask[:, None]).astype(jnp.bfloat16)


def per_device(
    element_attribute_table,
    active_group_tally,
    group_destination_part,
    element_vertex_permutation,
    softness_factor,
    entry_projection_coefficients,
    partition_score_coefficients,
    summary_query_key_coefficients,
    final_projection_coefficients,
):
    block_count, block_feature_rows = element_vertex_permutation.shape
    channels = element_attribute_table.shape[1]
    shard_count = lax.axis_size("pts")
    per_peer = max(1, (block_count + shard_count - 1) // shard_count)
    slot_total = shard_count * per_peer
    picking = (
        element_vertex_permutation[:, :, None]
        == jnp.arange(block_feature_rows, dtype=jnp.int32)[None, None, :]
    ).astype(jnp.bfloat16)
    blocks = jnp.einsum(
        "brk,bkc->brc",
        picking,
        element_attribute_table.reshape(block_count, block_feature_rows, channels),
        preferred_element_type=jnp.float32,
    ).astype(jnp.bfloat16)
    positions = jnp.arange(block_count, dtype=jnp.int32)
    block_live = positions < active_group_tally[0]
    earlier = (group_destination_part[:, None] == group_destination_part[None, :]) & (
        positions[None, :] < positions[:, None]
    )
    rank = jnp.sum(earlier.astype(jnp.int32), axis=1)
    slot_of_block = group_destination_part * per_peer + rank
    placing = (
        (slot_of_block[None, :] == jnp.arange(slot_total, dtype=jnp.int32)[:, None])
        & block_live[None, :]
    ).astype(jnp.bfloat16)
    slot_live = jnp.sum(placing, axis=1, dtype=jnp.float32)
    flags = (
        jnp.repeat(slot_live, block_feature_rows)
        .reshape(shard_count, per_peer * block_feature_rows)
        .astype(jnp.bfloat16)
    )
    flat = blocks.reshape(block_count, block_feature_rows * channels)
    placed = jnp.dot(placing, flat, preferred_element_type=jnp.float32).astype(jnp.bfloat16)
    arrived = lax.all_to_all(
        placed.reshape(shard_count, per_peer * block_feature_rows, channels),
        "pts",
        split_axis=0,
        concat_axis=0,
        tiled=True,
    )
    arrived_flags = lax.all_to_all(flags, "pts", split_axis=0, concat_axis=0, tiled=True)
    feature_matrix, middle_result = project_rows(
        arrived.reshape(-1, channels), entry_projection_coefficients
    )
    arrived, arrived_flags, feature_matrix, middle_result = (
        arrived,
        arrived_flags,
        feature_matrix.reshape(arrived.shape),
        middle_result.reshape(arrived.shape),
    )
    return finish_layer(
        arrived.reshape(-1, channels),
        feature_matrix.reshape(-1, channels),
        middle_result.reshape(-1, channels),
        arrived_flags.reshape(-1).astype(jnp.float32),
        block_feature_rows,
        softness_factor,
        partition_score_coefficients,
        summary_query_key_coefficients,
        final_projection_coefficients,
    )


def solution(mesh):
    placed = (
        P(("grp", "pts"), None),
        P(("grp", "pts")),
        P(("grp", "pts")),
        P(("grp", "pts"), None),
        P(),
        P(),
        P(),
        P(),
        P(),
    )
    return jax.shard_map(
        per_device, mesh=mesh, in_specs=placed, out_specs=P(("grp", "pts"), None), check_vma=False
    )
```

profile of v0, /device:TPU:8, one launch (start us, length us, event | category | flops | bytes accessed | tf_op | source)
XLA Modules:
  0.0 627.7 jit_solution(13447157429347500438)
XLA Ops:
  9.7 11.4 %all-to-all-start.1 = ((bf16[64,1,128]{2,1,0:T(2,128)(2,1)}), bf16[64,1,128]{2,1,0:T(2,128)(2,1)S(1)}, u32[]{:S(2)}, u32[]{:S(2)}) async-start(bf16[64,1,128]{2,1,0:T(2,128)(2,1)} %broadcast_in_dim.8), calls=%async_computation.1 | async-start | bytes 65536 | tf_op jit(solution)/shard_map/all_to_all | solution.py:149
  21.1 9.7 %convolution_convert_fusion.2 = bf16[64,128,512]{2,1,0:T(8,128)(2,1)} fusion(bf16[64,128,512]{2,1,0:T(8,128)(2,1)} %bitcast.78, s32[64,128]{1,0:T(8,128)} %param.14), kind=kOutput, calls=%fused_computation.30 | convolution fusion | flops 1078984704 | bytes 16809984 | tf_op jit(solution)/shard_map/brk,bkc->brc/dot_general | solution.py:117
  30.8 11.8 %copy.50 = bf16[8,8,128,512]{3,1,2,0:T(8,128)(2,1)} copy(bf16[8,8,128,512]{3,2,1,0:T(8,128)(2,1)} %bitcast.75) | data formatting | bytes 16777216
  42.6 9.1 %convolution_convert_fusion = bf16[64,65536]{1,0:T(8,128)(2,1)} fusion(bf16[64,65536]{1,0:T(8,128)(2,1)} %bitcast.73, s32[64]{0:T(128)S(1)} %add.32, pred[64]{0:T(512)(128)(4,1)S(1)} %iota_compare_fusion.4), kind=kOutput, calls=%fused_computation.10 | convolution fusion | flops 541073408 | bytes 16777536 | tf_op jit(solution)/shard_map/dot_general | solution.py:141
  51.7 9.9 %copy.51 = bf16[8,8,128,512]{3,2,1,0:T(8,128)(2,1)} copy(bf16[8,8,128,512]{3,1,2,0:T(8,128)(2,1)} %bitcast.74) | data formatting | bytes 16777216
  61.5 10.8 %all-to-all-start = ((bf16[64,128,512]{2,1,0:T(8,128)(2,1)}), bf16[64,128,512]{2,1,0:T(8,128)(2,1)}, u32[]{:S(2)}, u32[]{:S(2)}) async-start(bf16[64,128,512]{2,1,0:T(8,128)(2,1)} %bitcast.76), calls=%async_computation | async-start | bytes 16777216 | tf_op jit(solution)/shard_map/all_to_all | solution.py:142
  73.1 105.4 %all-to-all-done = bf16[64,128,512]{2,1,0:T(8,128)(2,1)} async-done(((bf16[64,128,512]{2,1,0:T(8,128)(2,1)}), bf16[64,128,512]{2,1,0:T(8,128)(2,1)}, u32[]{:S(2)}, u32[]{:S(2)}) %all-to-all-start) | async-done | bytes 8388640 | tf_op jit(solution)/shard_map/all_to_all | solution.py:142
  178.4 4.6 convert_reduce_fusion.1
  183.0 5.9 fusion.12
  188.9 5.2 fusion.14
  194.2 11.6 %convolution_convert_fusion.1 = bf16[8192,1024]{1,0:T(8,128)(2,1)} fusion(bf16[8192,512]{1,0:T(8,128)(2,1)S(1)} %fusion.14, bf16[512,1024]{1,0:T(8,128)(2,1)S(1)} %copy-done), kind=kOutput, calls=%fused_computation.28 | convolution fusion | flops 8598323200 | bytes 26214400 | tf_op jit(solution)/shard_map/dot_general | solution.py:21
  205.8 11.4 %fusion.54 = (bf16[8192,512]{1,0:T(8,128)(2,1)}, bf16[8192,512]{1,0:T(8,128)(2,1)}) fusion(bf16[8192,1024]{1,0:T(8,128)(2,1)} %convolution_convert_fusion.1), kind=kLoop, calls=%fused_computation.65 | loop fusion | bytes 33554432 | tf_op jit(solution)/shard_map/slice | solution.py:26
  217.2 21.2 %reshape.90 = bf16[8,1024,8,64]{3,2,1,0:T(8,128)(2,1)} reshape(bf16[8192,512]{1,0:T(8,128)(2,1)} %get-tuple-element.68) | data formatting | bytes 16777216 | tf_op jit(solution)/shard_map/reshape;reshape;reshape | solution.py:67
  238.4 18.3 %copy.34 = bf16[8,1024,8,64]{1,3,2,0:T(8,128)(2,1)} copy(bf16[8,1024,8,64]{3,2,1,0:T(8,128)(2,1)} %reshape.90) | data formatting | bytes 16777216 | tf_op jit(solution)/shard_map/while | solution.py:81
  256.8 47.9 %while.10 = (s32[]{:T(128)}, bf16[8,1024,8,256]{1,3,2,0:T(8,128)(2,1)}, bf16[8,1024,8,64]{1,3,2,0:T(8,128)(2,1)}, bf16[8,64,256]{2,1,0:T(8,128)(2,1)S(1)}, f32[8]{0:T(128)S(1)}, /*index=5*/s32[]{:T(128)}) while((s32[]{:T(128)}, bf16[8,1024,8,256]{1,3,2,0:T(8,128)(2,1)}, bf16[8,1024,8,64]{1,3,2,0:T(8,128)(2,1)}, ...), condition=%wide.region_5.0_spmd, body=%wide.region_3.5_spmd.sunk | while | flops 274735360 | bytes 30671972 | solution.py:81
  271.5 3.2 bitcast_dynamic-update-slice_fusion.2
  304.6 21.2 %reshape.91 = bf16[8,1024,8,64]{3,2,1,0:T(8,128)(2,1)} reshape(bf16[8192,512]{1,0:T(8,128)(2,1)} %get-tuple-element.69) | data formatting | bytes 16777216 | tf_op jit(solution)/shard_map/reshape;reshape;reshape | solution.py:83
  325.8 19.2 %fusion.24 = f32[8,256,64]{1,2,0:T(8,128)} fusion(bf16[8,1024,8,64]{3,2,1,0:T(8,128)(2,1)} %reshape.91, bf16[8,1024,8,256]{1,3,2,0:T(8,128)(2,1)} %get-tuple-element.32, bf16[8,1024]{1,0:T(8,128)(2,1)S(1)} %mul.34), kind=kOutput, calls=%fused_computation.37 | convolution fusion | flops 2164260864 | bytes 42483712 | tf_op jit(solution)/shard_map/nrhs,nrhd->hsd/dot_general | solution.py:84
  345.0 11.6 %convert_reduce_fusion = f32[8,256]{1,0:T(8,128)S(1)} fusion(bf16[8,1024,8,256]{1,3,2,0:T(8,128)(2,1)} %get-tuple-element.32, bf16[8,1024]{1,0:T(8,128)(2,1)S(1)} %mul.34), kind=kLoop, calls=%fused_computation.11 | loop fusion | flops 50329600 | bytes 33579008 | tf_op jit(solution)/shard_map/reduce_sum | solution.py:85
  356.6 200.8 %psum.15 = f32[8,256]{1,0:T(8,128)S(1)} all-reduce(f32[8,256]{1,0:T(8,128)S(1)} %convert_reduce_fusion), channel_id=1, replica_groups=mesh['grp'=2,'pts'=64] {'pts'}, use_global_device_ids=true, to_apply=%region_9.10 | all-reduce | flops 2048 | bytes 16384 | tf_op jit(solution)/shard_map/psum | solution.py:86
  563.2 18.2 %convert_bitcast_fusion = bf16[8,1024,8,64]{1,3,0,2:T(8,128)(2,1)} fusion(bf16[8,256,64,1]{1,2,3,0:T(8,128)(2,1)S(1)} %fusion.32, bf16[8,1024,8,256]{1,3,2,0:T(8,128)(2,1)} %get-tuple-element.32), kind=kOutput, calls=%fused_computation.29 | convolution fusion | flops 2151677952 | bytes 42205184 | tf_op jit(solution)/shard_map/nrhs,hsd->nrhd/dot_general | solution.py:89
  581.4 11.9 %copy.40 = bf16[8,1024,8,64]{1,0,3,2:T(8,128)(2,1)} copy(bf16[8,1024,8,64]{1,3,0,2:T(8,128)(2,1)} %convert_bitcast_fusion) | data formatting | bytes 16777216 | tf_op jit(solution)/shard_map/convert_element_type | solution.py:92
  593.3 16.6 %copy.52 = bf16[64,8,8,1024]{3,1,2,0:T(8,128)(2,1)} copy(bf16[64,8,8,1024]{3,2,1,0:T(8,128)(2,1)} %bitcast.77) | data formatting | bytes 16777216
  609.9 10.6 %fusion.16 = bf16[8192,512]{1,0:T(8,128)(2,1)} fusion(bf16[64,128,512]{2,1,0:T(8,128)(2,1)} %all-to-all-done, bf16[8192,512]{0,1:T(8,128)(2,1)} %bitcast.79, bf16[512,512]{1,0:T(8,128)(2,1)S(1)} %copy-done.4, f32[8192]{0:T(1024)S(1)} %bitcast.80), kind=kOutput, calls=%fused_computation.26 | convolution fusion | flops 4311744512 | bytes 25722880 | tf_op jit(solution)/shard_map/dot_general | solution.py:93
  (47 shorter events, 53.6 us)
Async XLA Ops:
  6.5 187.6 %copy-start = (bf16[512,1024]{1,0:T(8,128)(2,1)S(1)}, bf16[512,1024]{1,0:T(8,128)(2,1)}, u32[]{:S(2)}) copy-start(bf16[512,1024]{1,0:T(8,128)(2,1)} %param.16) | copy-start | bytes 3145732
  9.7 51.9 %all-to-all-start.1 = ((bf16[64,1,128]{2,1,0:T(2,128)(2,1)}), bf16[64,1,128]{2,1,0:T(2,128)(2,1)S(1)}, u32[]{:S(2)}, u32[]{:S(2)}) async-start(bf16[64,1,128]{2,1,0:T(2,128)(2,1)} %broadcast_in_dim.8), calls=%async_computation.1 | async-start | bytes 65536 | tf_op jit(solution)/shard_map/all_to_all | solution.py:149
  61.5 116.9 %all-to-all-start = ((bf16[64,128,512]{2,1,0:T(8,128)(2,1)}), bf16[64,128,512]{2,1,0:T(8,128)(2,1)}, u32[]{:S(2)}, u32[]{:S(2)}) async-start(bf16[64,128,512]{2,1,0:T(8,128)(2,1)} %bitcast.76), calls=%async_computation | async-start | bytes 16777216 | tf_op jit(solution)/shard_map/all_to_all | solution.py:142
  72.3 485.2 %all-reduce.2.cloned.1.call-start = ((), (), s32[]{:S(2)}) async-start(), calls=%async_computation.2 | async-start | bytes 1048576 | tf_op jit(solution)/shard_map/psum | solution.py:86
  238.4 18.3 %copy-start.5 = (bf16[8,64,256]{2,1,0:T(8,128)(2,1)S(1)}, bf16[8,64,256]{2,1,0:T(8,128)(2,1)}, u32[]{:S(2)}) copy-start(bf16[8,64,256]{2,1,0:T(8,128)(2,1)} %param.17) | copy-start | bytes 786436
  238.4 18.3 %copy-start.6 = (f32[8]{0:T(128)S(1)}, f32[8]{0:T(128)}, u32[]{:S(2)}) copy-start(f32[8]{0:T(128)} %param.15) | copy-start | bytes 100
  345.0 212.5 %copy-start.2 = (bf16[64,192]{1,0:T(8,128)(2,1)S(1)}, bf16[64,192]{1,0:T(8,128)(2,1)}, u32[]{:S(2)}) copy-start(bf16[64,192]{1,0:T(8,128)(2,1)} %param.18) | copy-start | bytes 73732
  593.3 16.6 %copy-start.3 = (f32[64,1,128]{2,1,0:T(1,128)S(1)}, f32[64,1,128]{2,1,0:T(1,128)}, u32[]{:S(2)}) copy-start(f32[64,1,128]{2,1,0:T(1,128)} %get-tuple-element.70) | copy-start | bytes 98308
  593.3 16.6 %copy-start.4 = (bf16[512,512]{1,0:T(8,128)(2,1)S(1)}, bf16[512,512]{1,0:T(8,128)(2,1)}, u32[]{:S(2)}) copy-start(bf16[512,512]{1,0:T(8,128)(2,1)} %param.19) | copy-start | bytes 1572868
  609.9 10.6 %copy-start.1 = (bf16[512,1024]{1,0:T(8,128)(2,1)S(1)}, bf16[512,1024]{1,0:T(8,128)(2,1)}, u32[]{:S(2)}) copy-start(bf16[512,1024]{1,0:T(8,128)(2,1)} %param.16) | copy-start | bytes 3145732
Sparse Core Ops, SparseCore 0:
  345.1 140.7 all-reduce.1
where the time goes:
time: 639 us; the launch traced here: 628 us
  blocking collectives  201 us (31%)
  local copies, waits for them, and re-layouts  123 us (19%)
  matrix products  107 us (17%)
  waiting for transfers between devices  105 us (16%)
  other arithmetic  55 us (9%)
  starting transfers between devices  22.2 us (3%)
  between operations  14.6 us (2%)
    psum x1, blocking collectives, finish_layer(): numer, denom = lax.psum((numer, denom), 'pts')  201 us
    all_to_all x1, waiting for transfers between devices, per_device(): lax.all_to_all(placed.reshape(shard_count, per_peer * block_feature_rows,...  105 us
    unnamed x17, local copies, waits for them, and re-layouts  38.2 us
    div x8, other arithmetic, weigh(): powered_entries / jnp.sum(powered_entries, axis=-1, keepdims=True)  25.3 us
    dot_general x8, matrix products, weigh(): jnp.einsum('rhd,hds->rhs', middle_part, partition_score_coefficients, pre...  22.5 us
    another operation x1, local copies, waits for them, and re-layouts, finish_layer(): middle_result.reshape(step_count, step_rows, head_count, head_width)  21.2 us
    another operation x1, local copies, waits for them, and re-layouts, finish_layer(): feature_matrix.reshape(step_count, step_rows, head_count, head_width)  21.2 us
    dot_general x1, matrix products, finish_layer(): jnp.einsum('nrhs,nrhd->hsd', masked, feature_steps, preferred_element_typ...  19.2 us
  transfers between devices with their start and end apart: 3, of which 1 were waited for; matrix products, arithmetic and copies ran while one was open for 8% of the time, Pallas kernels for 0%

commit v1 on v0

v1 whole, which is shorter than its diff:
```python
import functools

import jax
import jax.numpy as jnp
from jax import lax
from jax.experimental import pallas as pl
from jax.experimental.pallas import tpu as pltpu
from jax.sharding import PartitionSpec as P

F32 = jnp.float32
BF16 = jnp.bfloat16
MESH = pl.DeviceIdType.MESH
LOG2E = 1.4426950408889634
NORM_EPS = 1e-05
SLICE_EPS = 1e-05
HIGHEST = lax.Precision.HIGHEST
NT = (((1,), (1,)), ((), ()))
TN = (((0,), (0,)), ((), ()))

C = 512
HEADS = 8
S = 256
HD = 64
BLOCK = 128
BLOCKS = 64
PEERS = 64
SIDE = 4
STEP_ROWS = 1024
STEP_BLOCKS = STEP_ROWS // BLOCK
STEPS = BLOCKS * BLOCK // STEP_ROWS
ACC_ROWS = HD + 16
MSG_ROWS = 24
VMEM_LIMIT = 60 << 20


def whole(shape):
    return pl.BlockSpec(shape, lambda *_: (0,) * len(shape))


def normalize_rows(rows):
    values = rows.astype(F32)
    centred = values - jnp.mean(values, axis=-1, keepdims=True)
    spread = jnp.mean(centred * centred, axis=-1, keepdims=True)
    return (centred * lax.rsqrt(spread + NORM_EPS)).astype(BF16)


def head_weights(middle, score_ref, scale_ref, head):
    pair = middle[:, (head // 2) * 128 : (head // 2) * 128 + 128]
    scores = jnp.dot(pair, score_ref[head], preferred_element_type=F32)
    powered = jnp.exp2(scores * scale_ref[head])
    return (powered * (1.0 / jnp.sum(powered, axis=-1, keepdims=True))).astype(BF16)


def place_kernel(source_ref, table_ref, order_ref, placed_ref):
    rows = lax.broadcasted_iota(jnp.int32, (BLOCK, BLOCK), 0)

    @pl.loop(0, PEERS)
    def _(p):
        b = source_ref[p]
        picking = (order_ref[pl.ds(b, 1), :] == rows).astype(F32).astype(BF16)
        placed_ref[p] = lax.dot_general(
            picking, table_ref[b], TN, preferred_element_type=F32
        ).astype(BF16)


def place(source, table, order):
    return pl.pallas_call(
        place_kernel,
        name="place",
        out_shape=jax.ShapeDtypeStruct((PEERS, BLOCK, C), BF16),
        in_specs=[
            pl.BlockSpec(memory_space=pltpu.SMEM),
            pl.BlockSpec(memory_space=pltpu.VMEM),
            pl.BlockSpec(memory_space=pltpu.VMEM),
        ],
        out_specs=pl.BlockSpec(memory_space=pltpu.VMEM),
        compiler_params=pltpu.CompilerParams(vmem_limit_bytes=VMEM_LIMIT),
    )(source, table, order)


def sums_kernel(
    tally_ref, scale_ref, flag_ref, table_ref, feature_ref, middle_ref, score_ref, msg_ref, acc_ref
):
    step = pl.program_id(0)

    @pl.when(step == 0)
    def _():
        acc_ref[...] = jnp.zeros_like(acc_ref)

    normed = normalize_rows(table_ref[...])
    live = (
        lax.broadcasted_iota(jnp.int32, (1, STEP_ROWS), 1)
        < (tally_ref[0] - step * STEP_BLOCKS) * BLOCK
    ).astype(F32)
    features = lax.dot_general(feature_ref[...], normed, NT, preferred_element_type=F32)
    features = (features * live).astype(BF16)
    ones = jnp.broadcast_to(live, (16, STEP_ROWS)).astype(BF16)
    middle = jnp.dot(normed, middle_ref[...], preferred_element_type=F32).astype(BF16)
    for head in range(HEADS):
        weights = head_weights(middle, score_ref, scale_ref, head)
        left = jnp.concatenate([features[head * HD : head * HD + HD], ones], axis=0)
        acc_ref[head] += jnp.dot(left, weights, preferred_element_type=F32)

    @pl.when(step == pl.num_programs(0) - 1)
    def _():
        for p in range(PEERS):
            head, part = p // 8, (p % 8) * 8
            msg_ref[p, 0:8, :] = acc_ref[head, part : part + 8, 0:128]
            msg_ref[p, 8:16, :] = acc_ref[head, part : part + 8, 128:256]
            msg_ref[p, 16:17, :] = acc_ref[head, HD : HD + 1, 0:128]
            msg_ref[p, 17:18, :] = acc_ref[head, HD : HD + 1, 128:256]
        msg_ref[:, 18:24, :] = flag_ref[:, 0:6, :]


def partial_sums(tally, scale, flags, table, feature, middle, score):
    return pl.pallas_call(
        sums_kernel,
        name="partial_sums",
        grid=(STEPS,),
        out_shape=jax.ShapeDtypeStruct((PEERS, MSG_ROWS, 128), F32),
        in_specs=[
            pl.BlockSpec(memory_space=pltpu.SMEM),
            pl.BlockSpec(memory_space=pltpu.SMEM),
            whole((PEERS, 8, 128)),
            pl.BlockSpec((STEP_ROWS, C), lambda i: (i, 0)),
            whole((C, C)),
            whole((C, C)),
            whole((HEADS, 128, S)),
        ],
        out_specs=whole((PEERS, MSG_ROWS, 128)),
        scratch_shapes=[pltpu.VMEM((HEADS, ACC_ROWS, S), F32)],
        compiler_params=pltpu.CompilerParams(vmem_limit_bytes=VMEM_LIMIT),
        cost_estimate=pl.CostEstimate(
            flops=40_000_000_000, bytes_accessed=10_000_000, transcendentals=17_000_000
        ),
    )(tally, scale, flags, table, feature, middle, score)


def peer_at(me, r, sign):
    z, x, y = me // 16, (me // 4) % 4, me % 4
    dz, dx, dy = r // 16, (r // 4) % 4, r % 4
    return (
        ((z + sign * dz + SIDE) % SIDE) * 16
        + ((x + sign * dx + SIDE) % SIDE) * 4
        + (y + sign * dy + SIDE) % SIDE
    )


def reduce_kernel(
    msg_ref, tokens_ref, flags_ref, got_ref, mine_ref, send_sem, recv_sem, back_send, back_recv
):
    me = lax.axis_index("pts")
    barrier = pltpu.get_barrier_semaphore()

    @pl.loop(1, PEERS)
    def _(r):
        pl.semaphore_signal(
            barrier, inc=1, device_id={"pts": peer_at(me, r, 1)}, device_id_type=MESH
        )

    pl.semaphore_wait(barrier, PEERS - 1)

    def there(r):
        p = peer_at(me, r, 1)
        return pltpu.make_async_remote_copy(
            src_ref=msg_ref.at[p],
            dst_ref=got_ref.at[me],
            send_sem=send_sem.at[r],
            recv_sem=recv_sem.at[me],
            device_id={"pts": p},
            device_id_type=MESH,
        )

    def arriving(r):
        p = peer_at(me, r, -1)
        return pltpu.make_async_remote_copy(
            src_ref=msg_ref.at[p],
            dst_ref=got_ref.at[p],
            send_sem=send_sem.at[r],
            recv_sem=recv_sem.at[p],
            device_id={"pts": p},
            device_id_type=MESH,
        )

    @pl.loop(1, PEERS)
    def _(r):
        there(r).start()

    got_ref[me] = msg_ref[me]

    @pl.loop(1, PEERS)
    def _(r):
        arriving(r).wait_recv()

    total = lax.fori_loop(
        0, PEERS, lambda s, t: t + got_ref[s], jnp.zeros((MSG_ROWS, 128), F32)
    )
    mine_ref[0:8, :] = total[0:8] / (total[16:17] + SLICE_EPS)
    mine_ref[8:16, :] = total[8:16] / (total[17:18] + SLICE_EPS)

    def back(r):
        p = peer_at(me, r, 1)
        return pltpu.make_async_remote_copy(
            src_ref=mine_ref,
            dst_ref=tokens_ref.at[me],
            send_sem=back_send.at[r],
            recv_sem=back_recv.at[me],
            device_id={"pts": p},
            device_id_type=MESH,
        )

    def returning(r):
        p = peer_at(me, r, -1)
        return pltpu.make_async_remote_copy(
            src_ref=mine_ref,
            dst_ref=tokens_ref.at[p],
            send_sem=back_send.at[r],
            recv_sem=back_recv.at[p],
            device_id={"pts": p},
            device_id_type=MESH,
        )

    @pl.loop(1, PEERS)
    def _(r):
        back(r).start()

    flags_ref[...] = got_ref[:, 16:24, :]
    tokens_ref[me] = mine_ref[...]

    @pl.loop(1, PEERS)
    def _(r):
        returning(r).wait_recv()

    @pl.loop(1, PEERS)
    def _(r):
        there(r).wait_send()
        back(r).wait_send()


def reduce_tokens(msg):
    return pl.pallas_call(
        reduce_kernel,
        name="reduce_tokens",
        out_shape=(
            jax.ShapeDtypeStruct((PEERS, 16, 128), F32),
            jax.ShapeDtypeStruct((PEERS, 8, 128), F32),
        ),
        in_specs=[pl.BlockSpec(memory_space=pltpu.VMEM)],
        out_specs=[pl.BlockSpec(memory_space=pltpu.VMEM)] * 2,
        scratch_shapes=[
            pltpu.VMEM((PEERS, MSG_ROWS, 128), F32),
            pltpu.VMEM((16, 128), F32),
            pltpu.SemaphoreType.DMA((PEERS,)),
            pltpu.SemaphoreType.DMA((PEERS,)),
            pltpu.SemaphoreType.DMA((PEERS,)),
            pltpu.SemaphoreType.DMA((PEERS,)),
        ],
        compiler_params=pltpu.CompilerParams(
            collective_id=1, has_side_effects=True, vmem_limit_bytes=VMEM_LIMIT
        ),
        cost_estimate=pl.CostEstimate(
            flops=1_000_000, bytes_accessed=60_000_000, transcendentals=0
        ),
    )(msg)


def mix_tokens(tokens_ref, qkv_ref, mixed_ref):
    for head in range(HEADS):
        tokens = jnp.concatenate(
            [
                jnp.concatenate(
                    [tokens_ref[head * 8 + j, 0:8, :], tokens_ref[head * 8 + j, 8:16, :]], axis=1
                )
                for j in range(8)
            ],
            axis=0,
        )
        project = jnp.dot(qkv_ref[...], tokens, preferred_element_type=F32, precision=HIGHEST)
        queries = jnp.transpose(project[0:HD])
        scores = jnp.dot(
            queries, project[HD : 2 * HD], preferred_element_type=F32, precision=HIGHEST
        ) * (HD**-0.5)
        powered = jnp.exp(scores)
        attend = powered / jnp.sum(powered, axis=-1, keepdims=True)
        mixed = lax.dot_general(
            attend, project[2 * HD :], NT, preferred_element_type=F32, precision=HIGHEST
        )
        zeros = jnp.zeros_like(mixed)
        padded = [mixed, zeros] if head % 2 == 0 else [zeros, mixed]
        mixed_ref[head] = jnp.concatenate(padded, axis=1).astype(BF16)


def finish_kernel(
    scale_ref,
    tokens_ref,
    flags_ref,
    qkv_ref,
    rows_ref,
    middle_ref,
    score_ref,
    final_ref,
    out_ref,
    mixed_ref,
):
    step = pl.program_id(0)

    @pl.when(step == 0)
    def _():
        mix_tokens(tokens_ref, qkv_ref, mixed_ref)

    rows = rows_ref[...]
    middle = jnp.dot(
        normalize_rows(rows), middle_ref[...], preferred_element_type=F32
    ).astype(BF16)
    spread = []
    for pair in range(HEADS // 2):
        first = head_weights(middle, score_ref, scale_ref, 2 * pair)
        second = head_weights(middle, score_ref, scale_ref, 2 * pair + 1)
        spread.append(
            (
                jnp.dot(first, mixed_ref[2 * pair], preferred_element_type=F32)
                + jnp.dot(second, mixed_ref[2 * pair + 1], preferred_element_type=F32)
            ).astype(BF16)
        )
    spread = jnp.concatenate(spread, axis=1)
    update = jnp.dot(spread, final_ref[...], preferred_element_type=F32)
    for b in range(STEP_BLOCKS):
        flag = flags_ref[step * STEP_BLOCKS + b, 2:3, :]
        flag = jnp.concatenate([flag] * (C // 128), axis=1)
        part = slice(b * BLOCK, (b + 1) * BLOCK)
        out_ref[part, :] = ((rows[part].astype(F32) + update[part]) * flag).astype(BF16)


def finish(scale, tokens, flags, qkv, rows, middle, score, final):
    return pl.pallas_call(
        finish_kernel,
        name="finish",
        grid=(STEPS,),
        out_shape=jax.ShapeDtypeStruct((BLOCKS * BLOCK, C), BF16),
        in_specs=[
            pl.BlockSpec(memory_space=pltpu.SMEM),
            whole((PEERS, 16, 128)),
            whole((PEERS, 8, 128)),
            whole((3 * HD, HD)),
            pl.BlockSpec((STEP_ROWS, C), lambda i: (i, 0)),
            whole((C, C)),
            whole((HEADS, 128, S)),
            whole((C, C)),
        ],
        out_specs=pl.BlockSpec((STEP_ROWS, C), lambda i: (i, 0)),
        scratch_shapes=[pltpu.VMEM((HEADS, S, 128), BF16)],
        compiler_params=pltpu.CompilerParams(vmem_limit_bytes=VMEM_LIMIT),
        cost_estimate=pl.CostEstimate(
            flops=30_000_000_000, bytes_accessed=20_000_000, transcendentals=17_000_000
        ),
    )(scale, tokens, flags, qkv, rows, middle, score, final)


def per_device(table, tally, destination, order, softness, entry, score, qkv, final):
    slots = jnp.arange(BLOCKS, dtype=jnp.int32)
    hit = (destination[None, :] == slots[:, None]) & (slots[None, :] < tally[0])
    source = jnp.sum(jnp.where(hit, slots[None, :], 0), axis=1)
    flags = jnp.broadcast_to(
        jnp.sum(hit.astype(F32), axis=1)[:, None, None], (PEERS, 8, 128)
    )
    scale = LOG2E / softness
    empty = jnp.zeros((HEADS // 2, HD, S), BF16)
    score = jnp.stack(
        [
            jnp.concatenate([score[0::2], empty], axis=1),
            jnp.concatenate([empty, score[1::2]], axis=1),
        ],
        axis=1,
    ).reshape(HEADS, 2 * HD, S)
    feature = jnp.transpose(entry[:, :C])
    middle = entry[:, C:]
    qkv = jnp.transpose(qkv).astype(F32)

    placed = place(source, table.reshape(BLOCKS, BLOCK, C), order)
    arrived = lax.all_to_all(placed, "pts", split_axis=0, concat_axis=0, tiled=True)
    msg = partial_sums(tally, scale, flags, table, feature, middle, score)
    tokens, flags = reduce_tokens(msg)
    return finish(
        scale, tokens, flags, qkv, arrived.reshape(BLOCKS * BLOCK, C), middle, score, final
    )


def solution(mesh):
    split = P(("grp", "pts"))
    rows = P(("grp", "pts"), None)
    return jax.shard_map(
        per_device,
        mesh=mesh,
        in_specs=(rows, split, split, rows, P(), P(), P(), P(), P()),
        out_specs=rows,
        check_vma=False,
    )
```

time: 639 us -> 229 us (0.36)
  the two profiles are of different devices: /device:TPU:8 before, /device:TPU:16 now
where the time goes in v1:
time: 229 us; the launch traced here: 227 us
  Pallas kernels  209 us (91%)
  starting transfers between devices  11.6 us (5%)
  local copies, waits for them, and re-layouts  4.42 us (2%)
    pallas_call x1, Pallas kernels, reduce_tokens(): pl.pallas_call(reduce_kernel, name='reduce_tokens', out_shape=(jax.ShapeD...  93.6 us
    pallas_call x1, Pallas kernels, partial_sums(): pl.pallas_call(sums_kernel, name='partial_sums', grid=(STEPS,), out_shape...  47.7 us
    pallas_call x1, Pallas kernels, finish(): pl.pallas_call(finish_kernel, name='finish', grid=(STEPS,), out_shape=jax...  46.9 us
    pallas_call x1, Pallas kernels, place(): pl.pallas_call(place_kernel, name='place', out_shape=jax.ShapeDtypeStruct...  20.4 us
    all_to_all x1, starting transfers between devices, per_device(): lax.all_to_all(placed, 'pts', split_axis=0, concat_axis=0, tiled=True)  11.6 us
  transfers between devices with their start and end apart: 1, of which 0 were waited for; matrix products, arithmetic and copies ran while one was open for 2% of the time, Pallas kernels for 62%

profile of v1, /device:TPU:16, one launch (start us, length us, event | category | flops | bytes accessed | tf_op | source)
XLA Modules:
  0.0 227.3 jit_solution(16433662463727924202)
XLA Ops:
  0.7 1.3 select_reduce_fusion.source_ref
  1.9 20.4 %place.1 = bf16[64,128,512]{2,1,0:T(8,128)(2,1)} custom-call(s32[64]{0:T(128)} %select_reduce_fusion.source_ref, bf16[64,128,512]{2,1,0:T(8,128)(2,1)} %bitcast.11, s32[64,128]{1,0:T(8,128)} %order_ref.1), custom_call_target="tpu_custom_call" | custom-call | tf_op jit(solution)/shard_map/place/pallas_call | solution.py:67
  22.4 0.0 copy-start.1
  22.4 0.0 copy-start
  22.4 0.0 copy-start.2
  22.4 0.0 copy-start.4
  22.4 11.6 %all-to-all-start = ((bf16[64,128,512]{2,1,0:T(8,128)(2,1)}), bf16[64,128,512]{2,1,0:T(8,128)(2,1)}, u32[]{:S(2)}, u32[]{:S(2)}) async-start(bf16[64,128,512]{2,1,0:T(8,128)(2,1)} %place.1), calls=%async_computation | async-start | bytes 16777216 | tf_op jit(solution)/shard_map/all_to_all | solution.py:380
  34.1 0.0 copy-done.1
  34.1 0.1 pad_maximum_fusion
  34.2 0.8 copy.17
  35.0 0.0 copy-done
  35.0 0.9 fusion.1
  35.9 1.0 copy.19
  37.0 0.0 copy-done.2
  37.0 0.8 copy.18
  37.7 0.0 copy-done.3
  37.7 0.1 convert_reduce_fusion
  37.8 0.0 copy-done.4
  37.8 0.5 broadcast_divide_fusion.scale_ref
  38.4 0.8 broadcast_in_dim.14.flag_ref
  39.2 47.7 %partial_sums.1.msg_ref = f32[64,24,128]{2,1,0:T(8,128)} custom-call(s32[1]{0:T(128)} %copy.20.tally_ref, f32[8]{0:T(128)} %broadcast_divide_fusion.scale_ref, f32[64,8,128]{2,1,0:T(8,128)} %broadcast_in_dim.14.flag_ref, bf16[8192,512]{1,0:T(8,128)(2,1)} %table_ref.1, bf16[512,512]{1,0:T(8,128)(2,1)} %bitcast.14, ...), custom_call_target="tpu_custom_call" | custom-call | flops 40000000000 | bytes 10000000 | tf_op jit(solution)/shard_map/partial_sums/pallas_call | solution.py:116
  86.9 93.6 %reduce_tokens.1 = (f32[64,16,128]{2,1,0:T(8,128)}, f32[64,8,128]{2,1,0:T(8,128)}) custom-call(f32[64,24,128]{2,1,0:T(8,128)} %partial_sums.1.msg_ref), custom_call_target="tpu_custom_call" | custom-call | flops 1000000 | bytes 60000000 | tf_op jit(solution)/shard_map/reduce_tokens/pallas_call | solution.py:241
  180.4 0.0 all-to-all-done
  180.4 46.9 %finish.1 = bf16[8192,512]{1,0:T(8,128)(2,1)} custom-call(f32[8]{0:T(128)} %broadcast_divide_fusion.scale_ref, f32[64,16,128]{2,1,0:T(8,128)} %get-tuple-element.7.tokens_ref, f32[64,8,128]{2,1,0:T(8,128)} %get-tuple-element.8.flags_ref, f32[192,64]{1,0:T(8,128)} %bitcast.15, bf16[8192,512]{1,0:T(8,128)(2,1)} %bitcast.7.rows_ref, ...), custom_call_target="tpu_custom_call" | custom-call | flops 30000001024 | bytes 20000000 | tf_op jit(solution)/shard_map/finish/pallas_call | solution.py:335
  (4 shorter events, 0.1 us)
Async XLA Ops:
  22.4 11.7 %copy-start.1 = (bf16[8,64,256]{2,1,0:T(8,128)(2,1)S(1)}, bf16[8,64,256]{2,1,0:T(8,128)(2,1)}, u32[]{:S(2)}) copy-start(bf16[8,64,256]{2,1,0:T(8,128)(2,1)} %param.15) | copy-start | bytes 786436
  22.4 12.6 %copy-start = (bf16[512,1024]{1,0:T(8,128)(2,1)S(1)}, bf16[512,1024]{1,0:T(8,128)(2,1)}, u32[]{:S(2)}) copy-start(bf16[512,1024]{1,0:T(8,128)(2,1)} %param.14) | copy-start | bytes 3145732
  22.4 14.6 %copy-start.2 = (bf16[64,192]{1,0:T(8,128)(2,1)S(1)}, bf16[64,192]{1,0:T(8,128)(2,1)}, u32[]{:S(2)}) copy-start(bf16[64,192]{1,0:T(8,128)(2,1)} %param.16) | copy-start | bytes 73732
  22.4 15.3 %copy-start.3 = (s32[64]{0:T(128)S(1)}, s32[64]{0:T(128)}, u32[]{:S(2)}) copy-start(s32[64]{0:T(128)} %param.11) | copy-start | bytes 772
  22.4 15.4 %copy-start.4 = (f32[8]{0:T(128)S(1)}, f32[8]{0:T(128)}, u32[]{:S(2)}) copy-start(f32[8]{0:T(128)} %param.13) | copy-start | bytes 100
  22.4 158.0 %all-to-all-start = ((bf16[64,128,512]{2,1,0:T(8,128)(2,1)}), bf16[64,128,512]{2,1,0:T(8,128)(2,1)}, u32[]{:S(2)}, u32[]{:S(2)}) async-start(bf16[64,128,512]{2,1,0:T(8,128)(2,1)} %place.1), calls=%async_computation | async-start | bytes 16777216 | tf_op jit(solution)/shard_map/all_to_all | solution.py:380

commit v2 on v1

v2 whole, which is shorter than its diff:
```python
import functools

import jax
import jax.numpy as jnp
from jax import lax
from jax.experimental import pallas as pl
from jax.experimental.pallas import tpu as pltpu
from jax.sharding import PartitionSpec as P

F32 = jnp.float32
BF16 = jnp.bfloat16
MESH = pl.DeviceIdType.MESH
LOG2E = 1.4426950408889634
NORM_EPS = 1e-05
SLICE_EPS = 1e-05
HIGHEST = lax.Precision.HIGHEST
NT = (((1,), (1,)), ((), ()))
TN = (((0,), (0,)), ((), ()))

C = 512
HEADS = 8
S = 256
HD = 64
BLOCK = 128
BLOCKS = 64
PEERS = 64
SIDE = 4
STEP_ROWS = 1024
STEP_BLOCKS = STEP_ROWS // BLOCK
STEPS = BLOCKS * BLOCK // STEP_ROWS
ACC_ROWS = HD + 16
MSG_ROWS = 24
VMEM_LIMIT = 60 << 20
SEND_STEP = 4
SEND_REDUCE = 10


def whole(shape):
    return pl.BlockSpec(shape, lambda *_: (0,) * len(shape))


def normalize_rows(rows):
    values = rows.astype(F32)
    centred = values - jnp.mean(values, axis=-1, keepdims=True)
    spread = jnp.mean(centred * centred, axis=-1, keepdims=True)
    return (centred * lax.rsqrt(spread + NORM_EPS)).astype(BF16)


def head_weights(middle, score_ref, scale_ref, head):
    pair = middle[:, (head // 2) * 128 : (head // 2) * 128 + 128]
    scores = jnp.dot(pair, score_ref[head], preferred_element_type=F32)
    powered = jnp.exp2(scores * scale_ref[head])
    return (powered * (1.0 / jnp.sum(powered, axis=-1, keepdims=True))).astype(BF16)


def mix_tokens(tokens_ref, qkv_ref, mixed_ref):
    for head in range(HEADS):
        tokens = jnp.concatenate(
            [
                jnp.concatenate(
                    [tokens_ref[head * 8 + j, 0:8, :], tokens_ref[head * 8 + j, 8:16, :]], axis=1
                )
                for j in range(8)
            ],
            axis=0,
        )
        project = jnp.dot(qkv_ref[...], tokens, preferred_element_type=F32, precision=HIGHEST)
        queries = jnp.transpose(project[0:HD])
        scores = jnp.dot(
            queries, project[HD : 2 * HD], preferred_element_type=F32, precision=HIGHEST
        ) * (HD**-0.5)
        powered = jnp.exp(scores)
        attend = powered / jnp.sum(powered, axis=-1, keepdims=True)
        mixed = lax.dot_general(
            attend, project[2 * HD :], NT, preferred_element_type=F32, precision=HIGHEST
        )
        zeros = jnp.zeros_like(mixed)
        padded = [mixed, zeros] if head % 2 == 0 else [zeros, mixed]
        mixed_ref[head] = jnp.concatenate(padded, axis=1).astype(BF16)


def peer_at(me, i, sign):
    z, x, y = me // 16, (me // 4) % 4, me % 4
    a, b, c = i % 4, (i // 4) % 4, i // 16
    return (
        ((z + sign * a + 8) % SIDE) * 16
        + ((x + sign * (a + b) + 8) % SIDE) * 4
        + (y + sign * (a + c) + 8) % SIDE
    )


def layer_kernel(
    source_ref,
    tally_ref,
    scale_ref,
    table_hbm,
    order_ref,
    flag_ref,
    feature_ref,
    middle_ref,
    score_ref,
    qkv_ref,
    final_ref,
    out_hbm,
    table_ref,
    outgoing_ref,
    arrived_ref,
    done_ref,
    acc_ref,
    msg_ref,
    got_ref,
    mine_ref,
    tokens_ref,
    mixed_ref,
    load_sem,
    store_sem,
    block_send,
    block_recv,
    sum_send,
    sum_recv,
    token_send,
    token_recv,
):
    me = lax.axis_index("pts")
    barrier = pltpu.get_barrier_semaphore()
    load = pltpu.make_async_copy(table_hbm, table_ref, load_sem)
    load.start()

    @pl.loop(1, PEERS)
    def _(i):
        pl.semaphore_signal(
            barrier, inc=1, device_id={"pts": peer_at(me, i, 1)}, device_id_type=MESH
        )

    def copy(src, dst, send, recv, i):
        return pltpu.make_async_remote_copy(
            src_ref=src,
            dst_ref=dst,
            send_sem=send.at[i],
            recv_sem=recv.at[i],
            device_id={"pts": peer_at(me, i, 1)},
            device_id_type=MESH,
        )

    def block_copy(i):
        return copy(outgoing_ref.at[i], arrived_ref.at[i], block_send, block_recv, i)

    def sum_copy(i):
        return copy(msg_ref.at[peer_at(me, i, 1)], got_ref.at[i], sum_send, sum_recv, i)

    def token_copy(i):
        return copy(mine_ref, tokens_ref.at[me], token_send, token_recv, i)

    def token_arrival(i):
        return copy(mine_ref, tokens_ref.at[peer_at(me, i, -1)], token_send, token_recv, i)

    rows = lax.broadcasted_iota(jnp.int32, (BLOCK, BLOCK), 0)

    def placed(i):
        b = source_ref[peer_at(me, i, 1)]
        picking = (order_ref[b] == rows).astype(F32).astype(BF16)
        return lax.dot_general(picking, table_ref[b], TN, preferred_element_type=F32).astype(
            BF16
        )

    def place(first, count):
        for j in range(count):
            outgoing_ref[first + j] = placed(first + j)

    def send(first, count):
        @pl.loop(first, first + count)
        def _(i):
            block_copy(i).start()

    load.wait()
    place(1, SEND_STEP)
    pl.semaphore_wait(barrier, PEERS - 1)
    acc_ref[...] = jnp.zeros_like(acc_ref)

    @pl.loop(0, STEPS)
    def _(step):
        first = 1 + step * SEND_STEP
        send(first, SEND_STEP)
        place(first + SEND_STEP, SEND_STEP)
        part = table_ref[pl.ds(step * STEP_BLOCKS, STEP_BLOCKS)].reshape(STEP_ROWS, C)
        normed = normalize_rows(part)
        live = (
            lax.broadcasted_iota(jnp.int32, (1, STEP_ROWS), 1)
            < (tally_ref[0] - step * STEP_BLOCKS) * BLOCK
        ).astype(F32)
        features = lax.dot_general(feature_ref[...], normed, NT, preferred_element_type=F32)
        features = (features * live).astype(BF16)
        ones = jnp.broadcast_to(live, (16, STEP_ROWS)).astype(BF16)
        middle = jnp.dot(normed, middle_ref[...], preferred_element_type=F32).astype(BF16)
        for head in range(HEADS):
            weights = head_weights(middle, score_ref, scale_ref, head)
            left = jnp.concatenate([features[head * HD : head * HD + HD], ones], axis=0)
            acc_ref[head] += jnp.dot(left, weights, preferred_element_type=F32)

    for p in range(PEERS):
        head, part = p // 8, (p % 8) * 8
        msg_ref[p, 0:8, :] = acc_ref[head, part : part + 8, 0:128]
        msg_ref[p, 8:16, :] = acc_ref[head, part : part + 8, 128:256]
        msg_ref[p, 16:17, :] = acc_ref[head, HD : HD + 1, 0:128]
        msg_ref[p, 17:18, :] = acc_ref[head, HD : HD + 1, 128:256]
    msg_ref[:, 18:24, :] = flag_ref[:, 0:6, :]

    sent = 1 + STEPS * SEND_STEP
    ready = sent + SEND_STEP
    arrived_ref[0] = placed(0)

    @pl.loop(ready, PEERS)
    def _(i):
        outgoing_ref[i] = placed(i)

    @pl.loop(1, PEERS)
    def _(i):
        sum_copy(i).start()

    send(sent, SEND_REDUCE)
    got_ref[0] = msg_ref[me]

    def add(i, total):
        sum_copy(i).wait_recv()
        return total + got_ref[i]

    total = lax.fori_loop(1, PEERS, add, got_ref[0])
    mine_ref[0:8, :] = total[0:8] / (total[16:17] + SLICE_EPS)
    mine_ref[8:16, :] = total[8:16] / (total[17:18] + SLICE_EPS)
    tokens_ref[me] = mine_ref[...]

    @pl.loop(1, PEERS)
    def _(i):
        token_copy(i).start()

    send(sent + SEND_REDUCE, PEERS - sent - SEND_REDUCE)

    @pl.loop(1, PEERS)
    def _(i):
        token_arrival(i).wait_recv()

    mix_tokens(tokens_ref, qkv_ref, mixed_ref)

    def store(step, j):
        slot = step % 2
        return pltpu.make_async_copy(
            done_ref.at[slot, j],
            out_hbm.at[peer_at(me, step * STEP_BLOCKS + j, -1)],
            store_sem.at[slot, j],
        )

    @pl.loop(0, STEPS)
    def _(step):
        for j in range(STEP_BLOCKS):
            i = step * STEP_BLOCKS + j

            @pl.when(i > 0)
            def _():
                block_copy(i).wait_recv()

        @pl.when(step >= 2)
        def _():
            for j in range(STEP_BLOCKS):
                store(step - 2, j).wait()

        block_rows = arrived_ref[pl.ds(step * STEP_BLOCKS, STEP_BLOCKS)].reshape(STEP_ROWS, C)
        middle = jnp.dot(
            normalize_rows(block_rows), middle_ref[...], preferred_element_type=F32
        ).astype(BF16)
        spread = []
        for pair in range(HEADS // 2):
            first = head_weights(middle, score_ref, scale_ref, 2 * pair)
            second = head_weights(middle, score_ref, scale_ref, 2 * pair + 1)
            spread.append(
                (
                    jnp.dot(first, mixed_ref[2 * pair], preferred_element_type=F32)
                    + jnp.dot(second, mixed_ref[2 * pair + 1], preferred_element_type=F32)
                ).astype(BF16)
            )
        spread = jnp.concatenate(spread, axis=1)
        update = jnp.dot(spread, final_ref[...], preferred_element_type=F32)
        for j in range(STEP_BLOCKS):
            flag = got_ref[step * STEP_BLOCKS + j, 18:19, :]
            flag = jnp.concatenate([flag] * (C // 128), axis=1)
            part = slice(j * BLOCK, (j + 1) * BLOCK)
            done_ref[step % 2, j] = (
                (block_rows[part].astype(F32) + update[part]) * flag
            ).astype(BF16)
        for j in range(STEP_BLOCKS):
            store(step, j).start()

    for step in (STEPS - 2, STEPS - 1):
        for j in range(STEP_BLOCKS):
            store(step, j).wait()

    @pl.loop(1, PEERS)
    def _(i):
        block_copy(i).wait_send()
        sum_copy(i).wait_send()
        token_copy(i).wait_send()


def layer(source, tally, scale, table, order, flags, feature, middle, score, qkv, final):
    smem = pl.BlockSpec(memory_space=pltpu.SMEM)
    vmem = pl.BlockSpec(memory_space=pltpu.VMEM)
    hbm = pl.BlockSpec(memory_space=pl.ANY)
    dma = pltpu.SemaphoreType.DMA
    return pl.pallas_call(
        layer_kernel,
        name="layer",
        out_shape=jax.ShapeDtypeStruct((BLOCKS, BLOCK, C), BF16),
        in_specs=[smem, smem, smem, hbm, vmem, vmem, vmem, vmem, vmem, vmem, vmem],
        out_specs=hbm,
        scratch_shapes=[
            pltpu.VMEM((BLOCKS, BLOCK, C), BF16),
            pltpu.VMEM((BLOCKS, BLOCK, C), BF16),
            pltpu.VMEM((BLOCKS, BLOCK, C), BF16),
            pltpu.VMEM((2, STEP_BLOCKS, BLOCK, C), BF16),
            pltpu.VMEM((HEADS, ACC_ROWS, S), F32),
            pltpu.VMEM((PEERS, MSG_ROWS, 128), F32),
            pltpu.VMEM((PEERS, MSG_ROWS, 128), F32),
            pltpu.VMEM((16, 128), F32),
            pltpu.VMEM((PEERS, 16, 128), F32),
            pltpu.VMEM((HEADS, S, 128), BF16),
            dma,
            dma((2, STEP_BLOCKS)),
            dma((PEERS,)),
            dma((PEERS,)),
            dma((PEERS,)),
            dma((PEERS,)),
            dma((PEERS,)),
            dma((PEERS,)),
        ],
        compiler_params=pltpu.CompilerParams(
            collective_id=1, has_side_effects=True, vmem_limit_bytes=VMEM_LIMIT
        ),
    )(source, tally, scale, table, order, flags, feature, middle, score, qkv, final)


def per_device(table, tally, destination, order, softness, entry, score, qkv, final):
    slots = jnp.arange(BLOCKS, dtype=jnp.int32)
    hit = (destination[None, :] == slots[:, None]) & (slots[None, :] < tally[0])
    source = jnp.sum(jnp.where(hit, slots[None, :], 0), axis=1)
    flags = jnp.broadcast_to(
        jnp.sum(hit.astype(F32), axis=1)[:, None, None], (PEERS, 8, 128)
    )
    scale = LOG2E / softness
    empty = jnp.zeros((HEADS // 2, HD, S), BF16)
    score = jnp.stack(
        [
            jnp.concatenate([score[0::2], empty], axis=1),
            jnp.concatenate([empty, score[1::2]], axis=1),
        ],
        axis=1,
    ).reshape(HEADS, 2 * HD, S)
    feature = jnp.transpose(entry[:, :C])
    middle = entry[:, C:]
    qkv = jnp.transpose(qkv).astype(F32)

    return layer(
        source,
        tally,
        scale,
        table.reshape(BLOCKS, BLOCK, C),
        order.reshape(BLOCKS, 1, BLOCK),
        flags,
        feature,
        middle,
        score,
        qkv,
        final,
    ).reshape(BLOCKS * BLOCK, C)


def solution(mesh):
    split = P(("grp", "pts"))
    rows = P(("grp", "pts"), None)
    return jax.shard_map(
        per_device,
        mesh=mesh,
        in_specs=(rows, split, split, rows, P(), P(), P(), P(), P()),
        out_specs=rows,
        check_vma=False,
    )
```

time: 229 us -> 195 us (0.85)
  the two profiles are of different devices: /device:TPU:16 before, /device:TPU:14 now
where the time goes in v2:
time: 195 us
  Pallas kernels  176 us (90%)
  local copies, waits for them, and re-layouts  14.7 us (8%)
  other arithmetic  3.31 us (2%)
    pallas_call x1, Pallas kernels, layer(): pl.pallas_call(layer_kernel, name='layer', out_shape=jax.ShapeDtypeStruct...  176 us
    unnamed x2, local copies, waits for them, and re-layouts  8.37 us

profile of v2, /device:TPU:14, one launch (start us, length us, event | category | flops | bytes accessed | tf_op | source)
XLA Modules:
  0.0 194.7 jit_solution(7664727220737350240)
XLA Ops:
  0.7 0.8 convert_reduce_fusion
  1.4 1.3 select_reduce_fusion.source_ref
  2.7 1.2 broadcast_divide_fusion.scale_ref
  3.9 1.5 copy.18
  5.4 0.8 broadcast_in_dim.16.flag_ref
  6.3 1.0 fusion.2
  7.3 0.1 pad_maximum_fusion
  7.4 0.9 copy.17
  8.3 2.1 %fusion.1 = (bf16[512,512]{1,0:T(8,128)(2,1)}, bf16[512,512]{1,0:T(8,128)(2,1)S(1)}) fusion(bf16[512,1024]{1,0:T(8,128)(2,1)} %param.14), kind=kLoop, calls=%fused_computation.9 | loop fusion | bytes 2097152 | tf_op jit(solution)/shard_map/slice | solution.py:357
  10.3 1.1 copy.19
  11.4 176.0 %layer.1 = bf16[64,128,512]{2,1,0:T(8,128)(2,1)} custom-call(s32[64]{0:T(128)} %select_reduce_fusion.source_ref, s32[1]{0:T(128)} %copy.21.tally_ref, f32[8]{0:T(128)} %broadcast_divide_fusion.scale_ref, bf16[64,128,512]{2,1,0:T(8,128)(2,1)} %bitcast.13, s32[64,1,128]{2,1,0:T(1,128)} %bitcast.17, f32[64,8,128]{2,1,0:T(8,128)} %broadcast_in_dim.16.flag_ref, ...), custom_call_target="tpu_custom_call" | custom-call | tf_op jit(solution)/shard_map/layer/pallas_call | solution.py:308
  187.4 7.3 %copy.22 = bf16[8192,512]{1,0:T(8,128)(2,1)} copy(bf16[8192,512]{1,0:T(8,128)(2,1)} %bitcast.12) | data formatting | bytes 16777216
  (2 shorter events, 0.0 us)

commit v3 on v2

--- a/solution.py
+++ b/solution.py
@@ -1,5 +1,3 @@
-import functools
-
 import jax
 import jax.numpy as jnp
 from jax import lax
@@ -15,7 +13,6 @@
 SLICE_EPS = 1e-05
 HIGHEST = lax.Precision.HIGHEST
 NT = (((1,), (1,)), ((), ()))
-TN = (((0,), (0,)), ((), ()))
 
 C = 512
 HEADS = 8
@@ -32,7 +29,10 @@
 MSG_ROWS = 24
 VMEM_LIMIT = 60 << 20
 SEND_STEP = 4
-SEND_REDUCE = 10
+SEND_REDUCE = 4
+SEND_BATCH = 9
+EARLY = 2
+PREPARED = 4
 
 
 def whole(shape):
@@ -92,20 +92,25 @@
 def layer_kernel(
     source_ref,
     tally_ref,
-    scale_ref,
+    softness_ref,
+    destination_ref,
     table_hbm,
     order_ref,
-    flag_ref,
-    feature_ref,
-    middle_ref,
-    score_ref,
-    qkv_ref,
+    entry_ref,
+    score_in_ref,
+    qkv_in_ref,
     final_ref,
     out_hbm,
     table_ref,
     outgoing_ref,
     arrived_ref,
     done_ref,
+    weights_ref,
+    feature_ref,
+    score_ref,
+    qkv_ref,
+    scale_ref,
+    flag_ref,
     acc_ref,
     msg_ref,
     got_ref,
@@ -154,14 +159,13 @@
     def token_arrival(i):
         return copy(mine_ref, tokens_ref.at[peer_at(me, i, -1)], token_send, token_recv, i)
 
-    rows = lax.broadcasted_iota(jnp.int32, (BLOCK, BLOCK), 0)
+    columns = lax.broadcasted_iota(jnp.int32, (BLOCK, BLOCK), 1).astype(F32)
 
     def placed(i):
         b = source_ref[peer_at(me, i, 1)]
-        picking = (order_ref[b] == rows).astype(F32).astype(BF16)
-        return lax.dot_general(picking, table_ref[b], TN, preferred_element_type=F32).astype(
-            BF16
-        )
+        wanted = jnp.broadcast_to(order_ref[b].astype(F32), (BLOCK, BLOCK))
+        picking = (jnp.transpose(wanted) == columns).astype(F32).astype(BF16)
+        return jnp.dot(picking, table_ref[b], preferred_element_type=F32).astype(BF16)
 
     def place(first, count):
         for j in range(count):
@@ -172,10 +176,23 @@
         def _(i):
             block_copy(i).start()
 
+    feature_ref[...] = jnp.transpose(entry_ref[:, 0:C])
+    qkv_ref[...] = jnp.transpose(qkv_in_ref[...].astype(F32))
+    for head in range(HEADS):
+        own, other = (head % 2) * HD, (1 - head % 2) * HD
+        score_ref[head, own : own + HD, :] = score_in_ref[head]
+        score_ref[head, other : other + HD, :] = jnp.zeros((HD, S), BF16)
+        scale_ref[head] = LOG2E / jnp.full((1, S), softness_ref[head], F32)
+    slot = lax.broadcasted_iota(jnp.int32, (PEERS, BLOCKS), 1)
+    peer = lax.broadcasted_iota(jnp.int32, (PEERS, BLOCKS), 0)
+    hit = (destination_ref[...] == peer) & (slot < tally_ref[0])
+    flag_ref[...] = jnp.broadcast_to(
+        jnp.sum(hit.astype(F32), axis=1, keepdims=True), (PEERS, 128)
+    )
+    acc_ref[...] = jnp.zeros_like(acc_ref)
     load.wait()
     place(1, SEND_STEP)
     pl.semaphore_wait(barrier, PEERS - 1)
-    acc_ref[...] = jnp.zeros_like(acc_ref)
 
     @pl.loop(0, STEPS)
     def _(step):
@@ -191,7 +208,7 @@
         features = lax.dot_general(feature_ref[...], normed, NT, preferred_element_type=F32)
         features = (features * live).astype(BF16)
         ones = jnp.broadcast_to(live, (16, STEP_ROWS)).astype(BF16)
-        middle = jnp.dot(normed, middle_ref[...], preferred_element_type=F32).astype(BF16)
+        middle = jnp.dot(normed, entry_ref[:, C:], preferred_element_type=F32).astype(BF16)
         for head in range(HEADS):
             weights = head_weights(middle, score_ref, scale_ref, head)
             left = jnp.concatenate([features[head * HD : head * HD + HD], ones], axis=0)
@@ -203,21 +220,47 @@
         msg_ref[p, 8:16, :] = acc_ref[head, part : part + 8, 128:256]
         msg_ref[p, 16:17, :] = acc_ref[head, HD : HD + 1, 0:128]
         msg_ref[p, 17:18, :] = acc_ref[head, HD : HD + 1, 128:256]
-    msg_ref[:, 18:24, :] = flag_ref[:, 0:6, :]
+        msg_ref[p, 18:19, :] = flag_ref[p : p + 1, :]
+        msg_ref[p, 19:24, :] = jnp.zeros((5, 128), F32)
 
     sent = 1 + STEPS * SEND_STEP
     ready = sent + SEND_STEP
     arrived_ref[0] = placed(0)
 
-    @pl.loop(ready, PEERS)
-    def _(i):
-        outgoing_ref[i] = placed(i)
-
     @pl.loop(1, PEERS)
     def _(i):
         sum_copy(i).start()
 
     send(sent, SEND_REDUCE)
+    sent += SEND_REDUCE
+    place(ready, SEND_BATCH)
+    ready += SEND_BATCH
+
+    def wait_group(step):
+        for j in range(STEP_BLOCKS):
+            i = step * STEP_BLOCKS + j
+
+            @pl.when(i > 0)
+            def _():
+                block_copy(i).wait_recv()
+
+    def rows_of(step):
+        return arrived_ref[pl.ds(step * STEP_BLOCKS, STEP_BLOCKS)].reshape(STEP_ROWS, C)
+
+    def middle_of(step):
+        return jnp.dot(
+            normalize_rows(rows_of(step)), entry_ref[:, C:], preferred_element_type=F32
+        ).astype(BF16)
+
+    def prepare(first, last):
+        @pl.loop(first, last)
+        def _(step):
+            wait_group(step)
+            middle = middle_of(step)
+            for head in range(HEADS):
+                weights_ref[step, head] = head_weights(middle, score_ref, scale_ref, head)
+
+    prepare(0, EARLY)
     got_ref[0] = msg_ref[me]
 
     def add(i, total):
@@ -233,7 +276,14 @@
     def _(i):
         token_copy(i).start()
 
-    send(sent + SEND_REDUCE, PEERS - sent - SEND_REDUCE)
+    while ready < PEERS:
+        send(sent, ready - sent)
+        sent = ready
+        count = min(SEND_BATCH, PEERS - ready)
+        place(ready, count)
+        ready += count
+    send(sent, PEERS - sent)
+    prepare(EARLY, PREPARED)
 
     @pl.loop(1, PEERS)
     def _(i):
@@ -249,28 +299,16 @@
             store_sem.at[slot, j],
         )
 
-    @pl.loop(0, STEPS)
-    def _(step):
-        for j in range(STEP_BLOCKS):
-            i = step * STEP_BLOCKS + j
-
-            @pl.when(i > 0)
-            def _():
-                block_copy(i).wait_recv()
-
+    def finish(step, weights_of):
         @pl.when(step >= 2)
         def _():
             for j in range(STEP_BLOCKS):
                 store(step - 2, j).wait()
 
-        block_rows = arrived_ref[pl.ds(step * STEP_BLOCKS, STEP_BLOCKS)].reshape(STEP_ROWS, C)
-        middle = jnp.dot(
-            normalize_rows(block_rows), middle_ref[...], preferred_element_type=F32
-        ).astype(BF16)
+        block_rows = rows_of(step)
         spread = []
         for pair in range(HEADS // 2):
-            first = head_weights(middle, score_ref, scale_ref, 2 * pair)
-            second = head_weights(middle, score_ref, scale_ref, 2 * pair + 1)
+            first, second = weights_of(2 * pair), weights_of(2 * pair + 1)
             spread.append(
                 (
                     jnp.dot(first, mixed_ref[2 * pair], preferred_element_type=F32)
@@ -289,6 +327,16 @@
         for j in range(STEP_BLOCKS):
             store(step, j).start()
 
+    @pl.loop(0, PREPARED)
+    def _(step):
+        finish(step, lambda head: weights_ref[step, head])
+
+    @pl.loop(PREPARED, STEPS)
+    def _(step):
+        wait_group(step)
+        middle = middle_of(step)
+        finish(step, lambda head: head_weights(middle, score_ref, scale_ref, head))
+
     for step in (STEPS - 2, STEPS - 1):
         for j in range(STEP_BLOCKS):
             store(step, j).wait()
@@ -300,7 +348,7 @@
         token_copy(i).wait_send()
 
 
-def layer(source, tally, scale, table, order, flags, feature, middle, score, qkv, final):
+def layer(source, tally, softness, destination, table, order, entry, score, qkv, final):
     smem = pl.BlockSpec(memory_space=pltpu.SMEM)
     vmem = pl.BlockSpec(memory_space=pltpu.VMEM)
     hbm = pl.BlockSpec(memory_space=pl.ANY)
@@ -309,13 +357,19 @@
         layer_kernel,
         name="layer",
         out_shape=jax.ShapeDtypeStruct((BLOCKS, BLOCK, C), BF16),
-        in_specs=[smem, smem, smem, hbm, vmem, vmem, vmem, vmem, vmem, vmem, vmem],
+        in_specs=[smem, smem, smem, vmem, hbm, vmem, vmem, vmem, vmem, vmem],
         out_specs=hbm,
         scratch_shapes=[
             pltpu.VMEM((BLOCKS, BLOCK, C), BF16),
             pltpu.VMEM((BLOCKS, BLOCK, C), BF16),
             pltpu.VMEM((BLOCKS, BLOCK, C), BF16),
             pltpu.VMEM((2, STEP_BLOCKS, BLOCK, C), BF16),
+            pltpu.VMEM((PREPARED, HEADS, STEP_ROWS, S), BF16),
+            pltpu.VMEM((C, C), BF16),
+            pltpu.VMEM((HEADS, 2 * HD, S), BF16),
+            pltpu.VMEM((3 * HD, HD), F32),
+            pltpu.VMEM((HEADS, 1, S), F32),
+            pltpu.VMEM((PEERS, 128), F32),
             pltpu.VMEM((HEADS, ACC_ROWS, S), F32),
             pltpu.VMEM((PEERS, MSG_ROWS, 128), F32),
             pltpu.VMEM((PEERS, MSG_ROWS, 128), F32),
@@ -334,38 +388,21 @@
         compiler_params=pltpu.CompilerParams(
             collective_id=1, has_side_effects=True, vmem_limit_bytes=VMEM_LIMIT
         ),
-    )(source, tally, scale, table, order, flags, feature, middle, score, qkv, final)
+    )(source, tally, softness, destination, table, order, entry, score, qkv, final)
 
 
 def per_device(table, tally, destination, order, softness, entry, score, qkv, final):
     slots = jnp.arange(BLOCKS, dtype=jnp.int32)
     hit = (destination[None, :] == slots[:, None]) & (slots[None, :] < tally[0])
     source = jnp.sum(jnp.where(hit, slots[None, :], 0), axis=1)
-    flags = jnp.broadcast_to(
-        jnp.sum(hit.astype(F32), axis=1)[:, None, None], (PEERS, 8, 128)
-    )
-    scale = LOG2E / softness
-    empty = jnp.zeros((HEADS // 2, HD, S), BF16)
-    score = jnp.stack(
-        [
-            jnp.concatenate([score[0::2], empty], axis=1),
-            jnp.concatenate([empty, score[1::2]], axis=1),
-        ],
-        axis=1,
-    ).reshape(HEADS, 2 * HD, S)
-    feature = jnp.transpose(entry[:, :C])
-    middle = entry[:, C:]
-    qkv = jnp.transpose(qkv).astype(F32)
-
     return layer(
         source,
         tally,
-        scale,
+        softness,
+        destination.reshape(1, BLOCKS),
         table.reshape(BLOCKS, BLOCK, C),
         order.reshape(BLOCKS, 1, BLOCK),
-        flags,
-        feature,
-        middle,
+        entry,
         score,
         qkv,
         final,

time: 195 us -> 179 us (0.918)
  the two profiles are of different devices: /device:TPU:14 before, /device:TPU:6 now
where the time goes in v3:
time: 179 us; the launch traced here: 178 us
  Pallas kernels  169 us (94%)
  local copies, waits for them, and re-layouts  7.32 us (4%)
    pallas_call x1, Pallas kernels, layer(): pl.pallas_call(layer_kernel, name='layer', out_shape=jax.ShapeDtypeStruct...  169 us
    unnamed x1, local copies, waits for them, and re-layouts  7.32 us

profile of v3, /device:TPU:6, one launch (start us, length us, event | category | flops | bytes accessed | tf_op | source)
XLA Modules:
  0.0 178.3 jit_solution(18434303252995323173)
XLA Ops:
  0.7 1.3 select_reduce_fusion.source_ref
  1.9 169.0 %layer.1 = bf16[64,128,512]{2,1,0:T(8,128)(2,1)} custom-call(s32[64]{0:T(128)} %select_reduce_fusion.source_ref, s32[1]{0:T(128)} %copy.11.tally_ref, f32[8]{0:T(128)} %softness_ref.1, s32[1,64]{1,0:T(1,128)} %bitcast.9, bf16[64,128,512]{2,1,0:T(8,128)(2,1)} %bitcast.7, s32[64,1,128]{2,1,0:T(1,128)} %bitcast.8, bf16[512,1024]{1,0:T(8,128)(2,1)} %entry_ref.1, ...), custom_call_target="tpu_custom_call" | custom-call | tf_op jit(solution)/shard_map/layer/pallas_call | solution.py:356
  170.9 7.3 %copy.12 = bf16[8192,512]{1,0:T(8,128)(2,1)} copy(bf16[8192,512]{1,0:T(8,128)(2,1)} %bitcast.6) | data formatting | bytes 16777216
  (1 shorter events, 0.0 us)

commit v4 on v3

--- a/solution.py
+++ b/solution.py
@@ -28,8 +28,9 @@
 ACC_ROWS = HD + 16
 MSG_ROWS = 24
 VMEM_LIMIT = 60 << 20
-SEND_STEP = 4
-SEND_REDUCE = 4
+SEND_STEP = 8
+SEND_STEPS = 4
+SEND_REDUCE = 0
 SEND_BATCH = 9
 EARLY = 2
 PREPARED = 4
@@ -196,9 +197,12 @@
 
     @pl.loop(0, STEPS)
     def _(step):
-        first = 1 + step * SEND_STEP
-        send(first, SEND_STEP)
-        place(first + SEND_STEP, SEND_STEP)
+        @pl.when(step < SEND_STEPS)
+        def _():
+            first = 1 + step * SEND_STEP
+            send(first, SEND_STEP)
+            place(first + SEND_STEP, SEND_STEP)
+
         part = table_ref[pl.ds(step * STEP_BLOCKS, STEP_BLOCKS)].reshape(STEP_ROWS, C)
         normed = normalize_rows(part)
         live = (
@@ -223,7 +227,7 @@
         msg_ref[p, 18:19, :] = flag_ref[p : p + 1, :]
         msg_ref[p, 19:24, :] = jnp.zeros((5, 128), F32)
 
-    sent = 1 + STEPS * SEND_STEP
+    sent = 1 + SEND_STEPS * SEND_STEP
     ready = sent + SEND_STEP
     arrived_ref[0] = placed(0)
 
@@ -231,8 +235,9 @@
     def _(i):
         sum_copy(i).start()
 
-    send(sent, SEND_REDUCE)
-    sent += SEND_REDUCE
+    if SEND_REDUCE:
+        send(sent, SEND_REDUCE)
+        sent += SEND_REDUCE
     place(ready, SEND_BATCH)
     ready += SEND_BATCH
 

time: 179 us -> 160 us (0.89)
  the two profiles are of different devices: /device:TPU:6 before, /device:TPU:16 now
where the time goes in v4:
time: 160 us; the launch traced here: 159 us
  Pallas kernels  150 us (94%)
  local copies, waits for them, and re-layouts  7.32 us (5%)
    pallas_call x1, Pallas kernels, layer(): pl.pallas_call(layer_kernel, name='layer', out_shape=jax.ShapeDtypeStruct...  150 us
    unnamed x1, local copies, waits for them, and re-layouts  7.32 us

profile of v4, /device:TPU:16, one launch (start us, length us, event | category | flops | bytes accessed | tf_op | source)
XLA Modules:
  0.0 159.3 jit_solution(15401063254533158016)
XLA Ops:
  0.7 1.3 select_reduce_fusion.source_ref
  1.9 150.1 %layer.1 = bf16[64,128,512]{2,1,0:T(8,128)(2,1)} custom-call(s32[64]{0:T(128)} %select_reduce_fusion.source_ref, s32[1]{0:T(128)} %copy.11.tally_ref, f32[8]{0:T(128)} %softness_ref.1, s32[1,64]{1,0:T(1,128)} %bitcast.9, bf16[64,128,512]{2,1,0:T(8,128)(2,1)} %bitcast.7, s32[64,1,128]{2,1,0:T(1,128)} %bitcast.8, bf16[512,1024]{1,0:T(8,128)(2,1)} %entry_ref.1, ...), custom_call_target="tpu_custom_call" | custom-call | tf_op jit(solution)/shard_map/layer/pallas_call | solution.py:361
  152.0 7.3 %copy.12 = bf16[8192,512]{1,0:T(8,128)(2,1)} copy(bf16[8192,512]{1,0:T(8,128)(2,1)} %bitcast.6) | data formatting | bytes 16777216
  (1 shorter events, 0.0 us)

commit v5 on v4

--- a/solution.py
+++ b/solution.py
@@ -90,6 +90,117 @@
     )
 
 
+def finish_rows(block_rows, weights_of, mixed_ref, final_ref, flag_of, done_ref):
+    spread = []
+    for pair in range(HEADS // 2):
+        first, second = weights_of(2 * pair), weights_of(2 * pair + 1)
+        spread.append(
+            (
+                jnp.dot(first, mixed_ref[2 * pair], preferred_element_type=F32)
+                + jnp.dot(second, mixed_ref[2 * pair + 1], preferred_element_type=F32)
+            ).astype(BF16)
+        )
+    spread = jnp.concatenate(spread, axis=1)
+    update = jnp.dot(spread, final_ref[...], preferred_element_type=F32)
+    for j in range(block_rows.shape[0] // BLOCK):
+        flag = flag_of(j)
+        flag = jnp.concatenate([flag] * (C // 128), axis=1)
+        part = slice(j * BLOCK, (j + 1) * BLOCK)
+        done_ref[j] = ((block_rows[part].astype(F32) + update[part]) * flag).astype(BF16)
+
+
+def prepare_scores(score_in_ref, softness_ref, score_ref, scale_ref):
+    for head in range(HEADS):
+        own, other = (head % 2) * HD, (1 - head % 2) * HD
+        score_ref[head, own : own + HD, :] = score_in_ref[head]
+        score_ref[head, other : other + HD, :] = jnp.zeros((HD, S), BF16)
+        scale_ref[head] = LOG2E / jnp.full((1, S), softness_ref[head], F32)
+
+
+def settle_kernel(
+    softness_ref,
+    blocks_hbm,
+    mixed_ref,
+    flags_ref,
+    entry_ref,
+    score_in_ref,
+    final_ref,
+    out_hbm,
+    rows_ref,
+    score_ref,
+    scale_ref,
+    load_sem,
+    store_sem,
+):
+    me = lax.axis_index("pts")
+
+    def load(step):
+        part = pl.ds(step * STEP_BLOCKS, STEP_BLOCKS)
+        return pltpu.make_async_copy(blocks_hbm.at[part], rows_ref.at[part], load_sem.at[step])
+
+    def store(i):
+        return pltpu.make_async_copy(
+            rows_ref.at[i], out_hbm.at[peer_at(me, i, -1)], store_sem.at[i]
+        )
+
+    load(STEPS - 1).start()
+    for step in range(STEPS - 1):
+        load(step).start()
+    prepare_scores(score_in_ref, softness_ref, score_ref, scale_ref)
+    load(STEPS - 1).wait()
+    count = STEP_BLOCKS // 2
+    for half in range(2):
+        first = (STEPS - 1) * STEP_BLOCKS + half * count
+        block_rows = rows_ref[first : first + count].reshape(count * BLOCK, C)
+        middle = jnp.dot(
+            normalize_rows(block_rows), entry_ref[:, C:], preferred_element_type=F32
+        ).astype(BF16)
+        finish_rows(
+            block_rows,
+            lambda head: head_weights(middle, score_ref, scale_ref, head),
+            mixed_ref,
+            final_ref,
+            lambda j: flags_ref[first + j, 2:3, :],
+            rows_ref.at[pl.ds(first, count)],
+        )
+        if half == 0:
+            for step in range(STEPS - 1):
+                load(step).wait()
+
+                @pl.loop(step * STEP_BLOCKS, (step + 1) * STEP_BLOCKS)
+                def _(i):
+                    store(i).start()
+
+        @pl.loop(first, first + count)
+        def _(i):
+            store(i).start()
+
+    @pl.loop(0, BLOCKS)
+    def _(i):
+        store(i).wait()
+
+
+def settle(softness, blocks, mixed, flags, entry, score, final):
+    smem = pl.BlockSpec(memory_space=pltpu.SMEM)
+    vmem = pl.BlockSpec(memory_space=pltpu.VMEM)
+    hbm = pl.BlockSpec(memory_space=pl.ANY)
+    return pl.pallas_call(
+        settle_kernel,
+        name="settle",
+        out_shape=jax.ShapeDtypeStruct((BLOCKS, BLOCK, C), BF16),
+        in_specs=[smem, hbm, vmem, vmem, vmem, vmem, vmem],
+        out_specs=hbm,
+        scratch_shapes=[
+            pltpu.VMEM((BLOCKS, BLOCK, C), BF16),
+            pltpu.VMEM((HEADS, 2 * HD, S), BF16),
+            pltpu.VMEM((HEADS, 1, S), F32),
+            pltpu.SemaphoreType.DMA((STEPS,)),
+            pltpu.SemaphoreType.DMA((BLOCKS,)),
+        ],
+        compiler_params=pltpu.CompilerParams(vmem_limit_bytes=VMEM_LIMIT),
+    )(softness, blocks, mixed, flags, entry, score, final)
+
+
 def layer_kernel(
     source_ref,
     tally_ref,
@@ -102,6 +213,8 @@
     qkv_in_ref,
     final_ref,
     out_hbm,
+    mixed_hbm,
+    flags_hbm,
     table_ref,
     outgoing_ref,
     arrived_ref,
@@ -120,6 +233,7 @@
     mixed_ref,
     load_sem,
     store_sem,
+    extra_sem,
     block_send,
     block_recv,
     sum_send,
@@ -179,11 +293,7 @@
 
     feature_ref[...] = jnp.transpose(entry_ref[:, 0:C])
     qkv_ref[...] = jnp.transpose(qkv_in_ref[...].astype(F32))
-    for head in range(HEADS):
-        own, other = (head % 2) * HD, (1 - head % 2) * HD
-        score_ref[head, own : own + HD, :] = score_in_ref[head]
-        score_ref[head, other : other + HD, :] = jnp.zeros((HD, S), BF16)
-        scale_ref[head] = LOG2E / jnp.full((1, S), softness_ref[head], F32)
+    prepare_scores(score_in_ref, softness_ref, score_ref, scale_ref)
     slot = lax.broadcasted_iota(jnp.int32, (PEERS, BLOCKS), 1)
     peer = lax.broadcasted_iota(jnp.int32, (PEERS, BLOCKS), 0)
     hit = (destination_ref[...] == peer) & (slot < tally_ref[0])
@@ -296,61 +406,61 @@
 
     mix_tokens(tokens_ref, qkv_ref, mixed_ref)
 
-    def store(step, j):
-        slot = step % 2
+    share_mixed = pltpu.make_async_copy(mixed_ref, mixed_hbm, extra_sem.at[0])
+    share_flags = pltpu.make_async_copy(
+        got_ref.at[:, pl.ds(16, 8), :], flags_hbm, extra_sem.at[1]
+    )
+    share_flags.start()
+    share_mixed.start()
+
+    def store(step):
         return pltpu.make_async_copy(
-            done_ref.at[slot, j],
-            out_hbm.at[peer_at(me, step * STEP_BLOCKS + j, -1)],
-            store_sem.at[slot, j],
+            done_ref.at[step % 2],
+            out_hbm.at[pl.ds(step * STEP_BLOCKS, STEP_BLOCKS)],
+            store_sem.at[step % 2],
         )
 
     def finish(step, weights_of):
         @pl.when(step >= 2)
         def _():
-            for j in range(STEP_BLOCKS):
-                store(step - 2, j).wait()
-
-        block_rows = rows_of(step)
-        spread = []
-        for pair in range(HEADS // 2):
-            first, second = weights_of(2 * pair), weights_of(2 * pair + 1)
-            spread.append(
-                (
-                    jnp.dot(first, mixed_ref[2 * pair], preferred_element_type=F32)
-                    + jnp.dot(second, mixed_ref[2 * pair + 1], preferred_element_type=F32)
-                ).astype(BF16)
-            )
-        spread = jnp.concatenate(spread, axis=1)
-        update = jnp.dot(spread, final_ref[...], preferred_element_type=F32)
-        for j in range(STEP_BLOCKS):
-            flag = got_ref[step * STEP_BLOCKS + j, 18:19, :]
-            flag = jnp.concatenate([flag] * (C // 128), axis=1)
-            part = slice(j * BLOCK, (j + 1) * BLOCK)
-            done_ref[step % 2, j] = (
-                (block_rows[part].astype(F32) + update[part]) * flag
-            ).astype(BF16)
-        for j in range(STEP_BLOCKS):
-            store(step, j).start()
+            store(step - 2).wait()
+
+        finish_rows(
+            rows_of(step),
+            weights_of,
+            mixed_ref,
+            final_ref,
+            lambda j: got_ref[step * STEP_BLOCKS + j, 18:19, :],
+            done_ref.at[step % 2],
+        )
+        store(step).start()
 
     @pl.loop(0, PREPARED)
     def _(step):
         finish(step, lambda head: weights_ref[step, head])
 
-    @pl.loop(PREPARED, STEPS)
+    @pl.loop(PREPARED, STEPS - 1)
     def _(step):
         wait_group(step)
         middle = middle_of(step)
         finish(step, lambda head: head_weights(middle, score_ref, scale_ref, head))
 
-    for step in (STEPS - 2, STEPS - 1):
-        for j in range(STEP_BLOCKS):
-            store(step, j).wait()
+    wait_group(STEPS - 1)
+    last = pl.ds((STEPS - 1) * STEP_BLOCKS, STEP_BLOCKS)
+    rest = pltpu.make_async_copy(arrived_ref.at[last], out_hbm.at[last], extra_sem.at[2])
+    rest.start()
+    store(STEPS - 3).wait()
+    store(STEPS - 2).wait()
+    share_flags.wait()
+    share_mixed.wait()
 
     @pl.loop(1, PEERS)
     def _(i):
         block_copy(i).wait_send()
         sum_copy(i).wait_send()
         token_copy(i).wait_send()
+
+    rest.wait()
 
 
 def layer(source, tally, softness, destination, table, order, entry, score, qkv, final):
@@ -361,9 +471,13 @@
     return pl.pallas_call(
         layer_kernel,
         name="layer",
-        out_shape=jax.ShapeDtypeStruct((BLOCKS, BLOCK, C), BF16),
+        out_shape=(
+            jax.ShapeDtypeStruct((BLOCKS, BLOCK, C), BF16),
+            jax.ShapeDtypeStruct((HEADS, S, 128), BF16),
+            jax.ShapeDtypeStruct((PEERS, 8, 128), F32),
+        ),
         in_specs=[smem, smem, smem, vmem, hbm, vmem, vmem, vmem, vmem, vmem],
-        out_specs=hbm,
+        out_specs=[hbm, hbm, hbm],
         scratch_shapes=[
             pltpu.VMEM((BLOCKS, BLOCK, C), BF16),
             pltpu.VMEM((BLOCKS, BLOCK, C), BF16),
@@ -382,7 +496,8 @@
             pltpu.VMEM((PEERS, 16, 128), F32),
             pltpu.VMEM((HEADS, S, 128), BF16),
             dma,
-            dma((2, STEP_BLOCKS)),
+            dma((2,)),
+            dma((3,)),
             dma((PEERS,)),
             dma((PEERS,)),
             dma((PEERS,)),
@@ -400,7 +515,7 @@
     slots = jnp.arange(BLOCKS, dtype=jnp.int32)
     hit = (destination[None, :] == slots[:, None]) & (slots[None, :] < tally[0])
     source = jnp.sum(jnp.where(hit, slots[None, :], 0), axis=1)
-    return layer(
+    blocks, mixed, flags = layer(
         source,
         tally,
         softness,
@@ -411,7 +526,9 @@
         score,
         qkv,
         final,
-    ).reshape(BLOCKS * BLOCK, C)
+    )
+    settled = settle(softness, blocks, mixed, flags, entry, score, final)
+    return settled.reshape(BLOCKS * BLOCK, C)
 
 
 def solution(mesh):

time: 160 us -> 157 us (0.981)
  local copies, waits for them, and re-layouts: 7.32 us -> 0 us
  Pallas kernels: 150 us -> 155 us
    unnamed x1 -> x0, local copies, waits for them, and re-layouts: 7.32 us -> none
    pallas_call x1 -> x2, Pallas kernels: 150 us -> 155 us  [the longest x1 144 us: layer(): pl.pallas_call(layer_kernel, name='layer', out_shape=(jax.ShapeDtypeStruc...]
where the time goes in v5:
time: 157 us
  Pallas kernels  155 us (99%)
    pallas_call x1, Pallas kernels, layer(): pl.pallas_call(layer_kernel, name='layer', out_shape=(jax.ShapeDtypeStruc...  144 us
    pallas_call x1, Pallas kernels, settle(): pl.pallas_call(settle_kernel, name='settle', out_shape=jax.ShapeDtypeStru...  11 us

profile of v5, /device:TPU:16, one launch (start us, length us, event | category | flops | bytes accessed | tf_op | source)
XLA Modules:
  0.0 157.2 jit_solution(10415833588586725142)
XLA Ops:
  0.7 1.3 select_reduce_fusion.source_ref
  2.0 144.0 %layer.1 = (bf16[64,128,512]{2,1,0:T(8,128)(2,1)}, bf16[8,256,128]{2,1,0:T(8,128)(2,1)}, f32[64,8,128]{2,1,0:T(8,128)}) custom-call(s32[64]{0:T(128)} %select_reduce_fusion.source_ref, s32[1]{0:T(128)} %copy.10.tally_ref, f32[8]{0:T(128)} %softness_ref.3, s32[1,64]{1,0:T(1,128)} %bitcast.8, bf16[64,128,512]{2,1,0:T(8,128)(2,1)} %bitcast.6, ...), custom_call_target="tpu_custom_call" | custom-call | tf_op jit(solution)/shard_map/layer/pallas_call | solution.py:471
  146.0 11.0 %settle.1 = bf16[64,128,512]{2,1,0:T(8,128)(2,1)} custom-call(f32[8]{0:T(128)} %softness_ref.3, bf16[64,128,512]{2,1,0:T(8,128)(2,1)} %get-tuple-element.8.blocks_hbm, bf16[8,256,128]{2,1,0:T(8,128)(2,1)} %get-tuple-element.9.mixed_ref, f32[64,8,128]{2,1,0:T(8,128)} %get-tuple-element.10.flags_ref, bf16[512,1024]{1,0:T(8,128)(2,1)} %entry_ref.3, ...), custom_call_target="tpu_custom_call" | custom-call | tf_op jit(solution)/shard_map/settle/pallas_call | solution.py:187
  (1 shorter events, 0.0 us)

commit v6 on v5

--- a/solution.py
+++ b/solution.py
@@ -147,9 +147,16 @@
     for step in range(STEPS - 1):
         load(step).start()
     prepare_scores(score_in_ref, softness_ref, score_ref, scale_ref)
+    for step in range(STEPS - 1):
+        load(step).wait()
+
+        @pl.loop(step * STEP_BLOCKS, (step + 1) * STEP_BLOCKS)
+        def _(i):
+            store(i).start()
+
     load(STEPS - 1).wait()
-    count = STEP_BLOCKS // 2
-    for half in range(2):
+    count = STEP_BLOCKS
+    for half in range(1):
         first = (STEPS - 1) * STEP_BLOCKS + half * count
         block_rows = rows_ref[first : first + count].reshape(count * BLOCK, C)
         middle = jnp.dot(
@@ -163,14 +170,6 @@
             lambda j: flags_ref[first + j, 2:3, :],
             rows_ref.at[pl.ds(first, count)],
         )
-        if half == 0:
-            for step in range(STEPS - 1):
-                load(step).wait()
-
-                @pl.loop(step * STEP_BLOCKS, (step + 1) * STEP_BLOCKS)
-                def _(i):
-                    store(i).start()
-
         @pl.loop(first, first + count)
         def _(i):
             store(i).start()

time: 157 us -> 159 us (1.013)
  Pallas kernels: 155 us -> 157 us
    pallas_call x1, Pallas kernels: 11 us -> 12.9 us  [settle(): pl.pallas_call(settle_kernel, name='settle', out_shape=jax.ShapeDtypeStru...]
where the time goes in v6:
time: 159 us
  Pallas kernels  157 us (99%)
    pallas_call x1, Pallas kernels, layer(): pl.pallas_call(layer_kernel, name='layer', out_shape=(jax.ShapeDtypeStruc...  144 us
    pallas_call x1, Pallas kernels, settle(): pl.pallas_call(settle_kernel, name='settle', out_shape=jax.ShapeDtypeStru...  12.9 us

profile of v6, /device:TPU:16, one launch (start us, length us, event | category | flops | bytes accessed | tf_op | source)
XLA Modules:
  0.0 159.1 jit_solution(18156929766260081726)
XLA Ops:
  0.7 1.3 select_reduce_fusion.source_ref
  2.0 144.0 %layer.1 = (bf16[64,128,512]{2,1,0:T(8,128)(2,1)}, bf16[8,256,128]{2,1,0:T(8,128)(2,1)}, f32[64,8,128]{2,1,0:T(8,128)}) custom-call(s32[64]{0:T(128)} %select_reduce_fusion.source_ref, s32[1]{0:T(128)} %copy.10.tally_ref, f32[8]{0:T(128)} %softness_ref.3, s32[1,64]{1,0:T(1,128)} %bitcast.8, bf16[64,128,512]{2,1,0:T(8,128)(2,1)} %bitcast.6, ...), custom_call_target="tpu_custom_call" | custom-call | tf_op jit(solution)/shard_map/layer/pallas_call | solution.py:470
  145.9 12.9 %settle.1 = bf16[64,128,512]{2,1,0:T(8,128)(2,1)} custom-call(f32[8]{0:T(128)} %softness_ref.3, bf16[64,128,512]{2,1,0:T(8,128)(2,1)} %get-tuple-element.8.blocks_hbm, bf16[8,256,128]{2,1,0:T(8,128)(2,1)} %get-tuple-element.9.mixed_ref, f32[64,8,128]{2,1,0:T(8,128)} %get-tuple-element.10.flags_ref, bf16[512,1024]{1,0:T(8,128)(2,1)} %entry_ref.3, ...), custom_call_target="tpu_custom_call" | custom-call | tf_op jit(solution)/shard_map/settle/pallas_call | solution.py:186
  (1 shorter events, 0.0 us)
